TPU v7x, 512 devices: a whole 4x8x8 slice. The times are simulated.
512 devices in a mesh: dp: 16 (over y_hi, x), fsdp: 32 (over z, y_lo, core).
Axes of the slice: x: 4, y: 8 (y_hi: 4, y_lo: 2; y = y_hi * 2 + y_lo), z: 8, core: 2. Of those that a mesh axis runs over, the one named last changes fastest.
Arguments:
- tokens: bfloat16 [65536, 8192], P(('dp', 'fsdp')), may hold values from -6 to 6
- frozen_key_matrix: bfloat16 [8192, 512], P('fsdp'), may hold values from -0.0625 to 0.0625
- adapter_down_factor: float32 [96, 8192, 16], P('fsdp', 'dp'), may hold values from -0.0625 to 0.0625
- adapter_up_factor: float32 [96, 16, 512], P('fsdp', None, 'dp'), may hold values from -1.5 to 1.5
- key_norm_gain: float32 [128], replicated, may hold values from 0.1 to 1.9
- adapter_offset: int32 [16, 32], P('dp', 'fsdp'), may hold values from 0 to 2, as said below
- loss_row_count: int32 [16, 32], P('dp', 'fsdp'), may hold values from 32 to 128, as said below
- cotangent: bfloat16 [65536, 512], P(('dp', 'fsdp')), may hold values from -6 to 6
Outputs:
- keys: bfloat16 [65536, 512], P(('dp', 'fsdp'))
- input_grad: bfloat16 [65536, 8192], P(('dp', 'fsdp'))
- down_grad: float32 [96, 8192, 16], P('fsdp', 'dp')
- up_factor_gradient: float32 [96, 16, 512], P('fsdp', None, 'dp')
Inputs may be any that keep to these rules, and one draw needn't show every extreme that they name: `adapter_offset`: in every column j, each offset 0 to 2 is named by at least one dp index. `loss_row_count`: some block has 128 live rows and some block 32.
All inputs are finite; a program needn't handle non-finite values.
Results may differ from a plain program's by a relative error of at most 0.0033.
Values may be sent and summed in bfloat16 or wider, within the bound.
A program may use at most 64 MiB of HBM per device.

v0:
```python
import jax
import jax.numpy as jnp
from jax import lax
from jax.sharding import PartitionSpec as P

HD = 128
adapter_scale = 2.0
norm_eps = 1e-06


def on_device(
    tokens,
    frozen_key_matrix,
    adapter_down_factor,
    adapter_up_factor,
    key_norm_gain,
    adapter_offset,
    loss_row_count,
    cotangent,
):
    highest_precision = lax.Precision.HIGHEST
    row_count = tokens.shape[0]
    key_width = frozen_key_matrix.shape[1]
    stored_values = adapter_down_factor.shape[0]
    slot_value = adapter_offset[0, 0]
    live_count = loss_row_count[0, 0]
    selector = jnp.arange(stored_values, dtype=jnp.int32) == slot_value
    counted = jnp.where(selector, live_count, 0)
    summed_rows = lax.psum(counted, "dp")
    adapter_total = jnp.sum(jnp.where(selector, summed_rows, 0)).astype(jnp.float32)
    down_whole, up_whole = (
        lax.all_gather(adapter_down_factor, "dp", axis=1, tiled=True),
        lax.all_gather(adapter_up_factor, "dp", axis=2, tiled=True),
    )
    down_projection = lax.dynamic_index_in_dim(down_whole, slot_value, 0, keepdims=False)
    up_projection = lax.dynamic_index_in_dim(up_whole, slot_value, 0, keepdims=False)
    weight = lax.all_gather(frozen_key_matrix, "fsdp", axis=0, tiled=True)
    frozen_output = jnp.dot(tokens, weight, preferred_element_type=jnp.float32)
    tokens_float = tokens.astype(jnp.float32)
    lowrank_output = jnp.dot(tokens_float, down_projection, precision=highest_precision)
    projected_keys = frozen_output + adapter_scale * jnp.dot(
        lowrank_output, up_projection, precision=highest_precision
    )
    shaped = projected_keys.reshape(row_count, -1, HD)
    mean_square = jnp.mean(shaped * shaped, axis=-1, keepdims=True)
    inverse_rms = lax.rsqrt(mean_square + norm_eps)
    normed = shaped * inverse_rms
    keys = (normed * key_norm_gain).reshape(row_count, key_width).astype(jnp.bfloat16)
    row_mask = (jnp.arange(row_count, dtype=jnp.int32) < live_count).astype(jnp.float32)
    row_grad = cotangent.astype(jnp.float32) * row_mask[:, None] * (row_count / adapter_total)
    scaled_grad = row_grad.reshape(normed.shape) * key_norm_gain
    along_norm = jnp.mean(scaled_grad * normed, axis=-1, keepdims=True)
    prenorm_gradient = (inverse_rms * (scaled_grad - normed * along_norm)).reshape(
        row_count, key_width
    )
    pre_grad_low = prenorm_gradient.astype(jnp.bfloat16)
    lowrank_gradient = adapter_scale * jnp.dot(
        prenorm_gradient, up_projection.T, precision=highest_precision
    )
    input_base = lax.dot_general(
        pre_grad_low, weight, (((1,), (1,)), ((), ())), preferred_element_type=jnp.float32
    )
    input_grad = (
        input_base + jnp.dot(lowrank_gradient, down_projection.T, precision=highest_precision)
    ).astype(jnp.bfloat16)
    down_grad = lax.dot_general(
        tokens_float, lowrank_gradient, (((0,), (0,)), ((), ())), precision=highest_precision
    )
    up_factor_gradient = adapter_scale * lax.dot_general(
        lowrank_output, prenorm_gradient, (((0,), (0,)), ((), ())), precision=highest_precision
    )
    selector_float = selector.astype(jnp.float32)
    down_terms = selector_float[:, None, None] * down_grad[None]
    up_terms = selector_float[:, None, None] * up_factor_gradient[None]
    down_sum, up_sum = (
        lax.psum_scatter(down_terms, "dp", scatter_dimension=1, tiled=True),
        lax.psum_scatter(up_terms, "dp", scatter_dimension=2, tiled=True),
    )
    return (keys, input_grad, down_sum, up_sum)


def solution(mesh):
    placed = (
        P(("dp", "fsdp"), None),
        P("fsdp", None),
        P("fsdp", "dp", None),
        P("fsdp", None, "dp"),
        P(),
        P("dp", "fsdp"),
        P("dp", "fsdp"),
        P(("dp", "fsdp"), None),
    )
    return jax.shard_map(
        on_device,
        mesh=mesh,
        in_specs=placed,
        out_specs=(
            P(("dp", "fsdp"), None),
            P(("dp", "fsdp"), None),
            P("fsdp", "dp", None),
            P("fsdp", None, "dp"),
        ),
        check_vma=False,
    )
```

profile of v0, /device:TPU:64, one launch (start us, length us, event | category | flops | bytes accessed | tf_op | source)
XLA Modules:
  0.0 360.2 jit_solution(965696795780993262)
XLA Ops:
  7.2 0.7 all-gather.5.cloned.1.call-update
  8.0 0.7 all-gather.3.cloned.1.call-update
  10.0 18.7 %psum.7 = s32[3]{0:T(128)S(1)} all-reduce(s32[3]{0:T(128)S(1)} %fusion.12), channel_id=1, replica_groups=mesh['dp'=16,'fsdp'=32] {'dp'}, use_global_device_ids=true, to_apply=%region_1.2 | all-reduce | flops 3 | bytes 24 | tf_op jit(solution)/shard_map/psum | solution.py:29
  28.7 0.8 copy.12
  29.5 0.6 select_reduce_fusion
  30.9 1.0 multiply_multiply_fusion
  32.0 55.4 %all_gather.11 = f32[3,16,512]{1,0,2:T(4,128)S(1)} all-gather(f32[3,16,32]{1,0,2:T(4,128)S(1)} %copy.12), channel_id=1, replica_groups=mesh['dp'=16,'fsdp'=32] {'dp'}, dimensions={2}, use_global_device_ids=true | all-gather | bytes 104448 | tf_op jit(solution)/shard_map/all_gather | solution.py:33
  87.7 2.8 fusion.3
  90.4 65.8 %all-gather.3.cloned.1.call-done = bf16[8192,512]{1,0:T(8,128)(2,1)} async-done(((bf16[256,512]{1,0:T(8,128)(2,1)}), bf16[8192,512]{1,0:T(8,128)(2,1)}) %all-gather.3.cloned.1.call-update) | async-done | bytes 8388624 | tf_op jit(solution)/shard_map/all_gather | solution.py:37
  156.2 4.6 %fusion.15 = f32[128,512]{1,0:T(8,128)S(1)} fusion(bf16[128,8192]{1,0:T(8,128)(2,1)S(1)} %copy-done, bf16[8192,512]{1,0:T(8,128)(2,1)} %all-gather.3.cloned.1.call-done), kind=kOutput, calls=%fused_computation.35 | convolution fusion | flops 1073741824 | bytes 10747904 | tf_op jit(solution)/shard_map/dot_general | solution.py:38
  160.9 0.4 fusion.1
  161.7 0.4 multiply_reduce_fusion
  162.5 0.7 fusion.8
  163.2 0.5 convolution_multiply_fusion.2
  164.0 1.7 convolution_bitcast_fusion
  165.8 0.4 copy.13
  166.2 1.1 reshape.49
  167.3 2.4 broadcast_multiply_fusion
  169.7 6.2 %fusion.9 = f32[128,8192]{1,0:T(8,128)S(1)} fusion(bf16[8192,512]{1,0:T(8,128)(2,1)} %all-gather.3.cloned.1.call-done, f32[128,512]{1,0:T(8,128)S(1)} %get-tuple-element.4), kind=kOutput, calls=%fused_computation.21 | convolution fusion | flops 1073807360 | bytes 12845056 | tf_op jit(solution)/shard_map/dot_general | solution.py:60
  175.9 5.9 %fusion = bf16[128,8192]{1,0:T(8,128)(2,1)} fusion(f32[128,8192]{1,0:T(8,128)S(1)} %fusion.9, f32[128,16]{0,1:T(8,128)S(1)} %convolution_multiply_fusion.2, f32[3,8192,16]{1,2,0:T(8,128)} %all-gather.5.cloned.1.call-done, s32[]{:T(128)S(6)} %select_n.14), kind=kOutput, calls=%fused_computation.1 | convolution fusion | flops 203423744 | bytes 6823940 | tf_op jit(solution)/shard_map/dot_general | solution.py:64
  181.8 76.3 %reduce-scatter.7.cloned.1.call-done = f32[32,48]{1,0:T(8,128)} async-done(((f32[512,48]{1,0:T(8,128)}), f32[32,48]{1,0:T(8,128)}) %reduce-scatter.7.cloned.1.call-update) | async-done | bytes 6160
  258.1 0.8 reshape.50
  258.9 0.7 copy.14
  259.6 94.1 %reduce-scatter.5.cloned.1.call-done = f32[3,512,16]{1,2,0:T(8,128)} async-done(((f32[3,8192,16]{1,2,0:T(8,128)}), f32[3,512,16]{1,2,0:T(8,128)}) %reduce-scatter.5.cloned.1.call-update) | async-done | bytes 98320 | tf_op jit(solution)/shard_map/reduce_scatter | solution.py:76
  (27 shorter events, 1.6 us)
Async XLA Ops:
  7.2 80.5 %copy-start = (bf16[128,8192]{1,0:T(8,128)(2,1)S(1)}, bf16[128,8192]{1,0:T(8,128)(2,1)}, u32[]{:S(2)}) copy-start(bf16[128,8192]{1,0:T(8,128)(2,1)} %param.8) | copy-start | bytes 6291460
  7.2 80.4 %copy-start.2 = (f32[128]{0:T(128)S(1)}, f32[128]{0:T(128)}, u32[]{:S(2)}) copy-start(f32[128]{0:T(128)} %param.12) | copy-start | bytes 1540
  7.2 80.4 %all-gather.5.cloned.1.call-start = ((), (), s32[]{:S(2)}) async-start(), calls=%async_computation.3 | async-start | bytes 1671168 | tf_op jit(solution)/shard_map/all_gather | solution.py:32
  7.9 148.3 %all-gather.3.cloned.1.call-start = ((), (), s32[]{:S(2)}) async-start(), calls=%async_computation.2 | async-start | bytes 8650752 | tf_op jit(solution)/shard_map/all_gather | solution.py:37
  8.7 249.4 %reduce-scatter.7.cloned.1.call-start = ((), (), s32[]{:S(2)}) async-start(), calls=%async_computation.5 | async-start | bytes 278528
  160.9 1.6 copy-start.1
  167.3 186.4 %reduce-scatter.5.cloned.1.call-start = ((), (), s32[]{:S(2)}) async-start(), calls=%async_computation.4 | async-start | bytes 1671168 | tf_op jit(solution)/shard_map/reduce_scatter | solution.py:76
Sparse Core Ops, SparseCore 0:
  11.0 70.9 all-gather.4
  84.2 72.0 all-gather.2
  167.4 90.6 reduce-scatter.6
  263.2 90.4 reduce-scatter.4
where the time goes:
time: 361 us; the launch traced here: 360 us
  waiting for transfers between devices  238 us (66%)
  blocking collectives  74.1 us (21%)
  matrix products  22.5 us (6%)
  between operations  15.9 us (4%)
  other arithmetic  5.37 us (1%)
  local copies, waits for them, and re-layouts  4.64 us (1%)
    reduce_scatter x1, waiting for transfers between devices, on_device(): lax.psum_scatter(down_terms, 'dp', scatter_dimension=1, tiled=True)  94.1 us
    unnamed x5, waiting for transfers between devices  77.7 us
    all_gather x1, waiting for transfers between devices, on_device(): weight = lax.all_gather(frozen_key_matrix, 'fsdp', axis=0, tiled=True)  65.8 us
    all_gather x1, blocking collectives, on_device(): lax.all_gather(adapter_up_factor, 'dp', axis=2, tiled=True)  55.4 us
    psum x1, blocking collectives, on_device(): summed_rows = lax.psum(counted, 'dp')  18.7 us
  transfers between devices with their start and end apart: 4, of which 3 were waited for; matrix products, arithmetic and copies ran while one was open for 6% of the time, Pallas kernels for 0%

commit v1 on v0

--- a/solution.py
+++ b/solution.py
@@ -34,7 +34,9 @@
     )
     down_projection = lax.dynamic_index_in_dim(down_whole, slot_value, 0, keepdims=False)
     up_projection = lax.dynamic_index_in_dim(up_whole, slot_value, 0, keepdims=False)
-    weight = lax.all_gather(frozen_key_matrix, "fsdp", axis=0, tiled=True)
+    weight = jnp.concatenate(
+        lax.all_to_all(jnp.stack([frozen_key_matrix] * lax.axis_size("fsdp")), "fsdp", 0, 0), axis=0
+    )
     frozen_output = jnp.dot(tokens, weight, preferred_element_type=jnp.float32)
     tokens_float = tokens.astype(jnp.float32)
     lowrank_output = jnp.dot(tokens_float, down_projection, precision=highest_precision)

time: 361 us -> 447 us (1.24)
  blocking collectives: 74.1 us -> 214 us
  waiting for transfers between devices: 238 us -> 169 us
  starting transfers between devices: 0.16 us -> 11.6 us
  local copies, waits for them, and re-layouts: 4.64 us -> 9.17 us
    psum x1, blocking collectives: 18.7 us -> 159 us  [on_device(): summed_rows = lax.psum(counted, 'dp')]
    all_gather x1 -> x0, waiting for transfers between devices: 65.8 us -> none  [on_device(): weight = lax.all_gather(frozen_key_matrix, 'fsdp', axis=0, tiled=True)]
    all_to_all x0 -> x1, starting transfers between devices: none -> 11.3 us  [on_device(): lax.all_to_all(jnp.stack([frozen_key_matrix] * lax.axis_size('fsdp')), 'f...]
    another operation x0 -> x1, local copies, waits for them, and re-layouts: none -> 5.25 us  [on_device(): jnp.stack([frozen_key_matrix] * lax.axis_size('fsdp'))]
    unnamed x5 -> x4, waiting for transfers between devices: 77.7 us -> 75.2 us
  transfers between devices with their start and end apart: 4 -> 4, of which waited for: 3 -> 2; matrix products, arithmetic and copies ran while one was open for 6% -> 4% of each run, Pallas kernels for 0% -> 0%
where the time goes in v1:
time: 447 us
  blocking collectives  214 us (48%)
  waiting for transfers between devices  169 us (38%)
  matrix products  22.4 us (5%)
  between operations  15.9 us (4%)
  starting transfers between devices  11.6 us (3%)
  local copies, waits for them, and re-layouts  9.17 us (2%)
  other arithmetic  4.55 us (1%)
    psum x1, blocking collectives, on_device(): summed_rows = lax.psum(counted, 'dp')  159 us
    reduce_scatter x1, waiting for transfers between devices, on_device(): lax.psum_scatter(down_terms, 'dp', scatter_dimension=1, tiled=True)  94.1 us
    unnamed x4, waiting for transfers between devices  75.2 us
    all_gather x1, blocking collectives, on_device(): lax.all_gather(adapter_up_factor, 'dp', axis=2, tiled=True)  54.3 us
    all_to_all x1, starting transfers between devices, on_device(): lax.all_to_all(jnp.stack([frozen_key_matrix] * lax.axis_size('fsdp')), 'f...  11.3 us
  transfers between devices with their start and end apart: 4, of which 2 were waited for; matrix products, arithmetic and copies ran while one was open for 4% of the time, Pallas kernels for 0%

profile of v1, /device:TPU:64, one launch (start us, length us, event | category | flops | bytes accessed | tf_op | source)
XLA Modules:
  0.0 446.8 jit_solution(6314250162842084171)
XLA Ops:
  7.2 5.3 %stack.2 = bf16[32,256,512]{2,1,0:T(8,128)(2,1)} broadcast(bf16[256,512]{1,0:T(8,128)(2,1)} %param.9), dimensions={1,2} | broadcast | bytes 8650752 | tf_op jit(solution)/shard_map/stack | solution.py:38
  12.4 11.3 %all-to-all-start = ((bf16[32,256,512]{2,1,0:T(8,128)(2,1)}), bf16[32,256,512]{2,1,0:T(8,128)(2,1)}, u32[]{:S(2)}, u32[]{:S(2)}) async-start(bf16[32,256,512]{2,1,0:T(8,128)(2,1)} %stack.2), calls=%async_computation | async-start | bytes 16777216 | tf_op jit(solution)/shard_map/all_to_all | solution.py:38
  23.8 0.7 all-gather.2.cloned.1.call-update
  25.9 159.4 %psum.7 = s32[3]{0:T(128)S(1)} all-reduce(s32[3]{0:T(128)S(1)} %fusion.12), channel_id=1, replica_groups=mesh['dp'=16,'fsdp'=32] {'dp'}, use_global_device_ids=true, to_apply=%region_1.2 | all-reduce | flops 3 | bytes 24 | tf_op jit(solution)/shard_map/psum | solution.py:29
  185.4 0.6 select_reduce_fusion
  186.9 54.3 %all_gather.7 = f32[3,16,512]{1,0,2:T(4,128)S(1)} all-gather(f32[3,16,32]{1,0,2:T(4,128)S(1)} %copy.12), channel_id=1, replica_groups=mesh['dp'=16,'fsdp'=32] {'dp'}, dimensions={2}, use_global_device_ids=true | all-gather | bytes 104448 | tf_op jit(solution)/shard_map/all_gather | solution.py:33
  241.2 0.2 constant_dynamic-slice_fusion
  241.5 2.8 fusion.3
  244.3 4.6 %fusion.15 = f32[128,512]{1,0:T(8,128)S(1)} fusion(bf16[128,8192]{1,0:T(8,128)(2,1)S(1)} %copy-done, bf16[8192,512]{1,0:T(8,128)(2,1)} %bitcast), kind=kOutput, calls=%fused_computation.35 | convolution fusion | flops 1073741824 | bytes 10747904 | tf_op jit(solution)/shard_map/dot_general | solution.py:40
  248.9 0.4 fusion.1
  249.7 0.4 multiply_reduce_fusion
  250.5 0.7 fusion.8
  251.2 0.5 convolution_multiply_fusion.2
  251.7 0.3 convolution_multiply_fusion.1
  252.0 1.7 convolution_bitcast_fusion
  253.8 0.4 copy.13
  254.2 1.1 reshape.55
  255.6 2.4 broadcast_multiply_fusion
  258.0 6.2 %fusion.9 = f32[128,8192]{1,0:T(8,128)S(1)} fusion(bf16[8192,512]{1,0:T(8,128)(2,1)} %bitcast, f32[128,512]{1,0:T(8,128)S(1)} %get-tuple-element.4), kind=kOutput, calls=%fused_computation.21 | convolution fusion | flops 1073807360 | bytes 12845056 | tf_op jit(solution)/shard_map/dot_general | solution.py:62
  264.2 5.9 %fusion = bf16[128,8192]{1,0:T(8,128)(2,1)} fusion(f32[128,8192]{1,0:T(8,128)S(1)} %fusion.9, f32[128,16]{0,1:T(8,128)S(1)} %convolution_multiply_fusion.2, f32[3,8192,16]{1,2,0:T(8,128)} %all-gather.2.cloned.1.call-done, s32[]{:T(128)S(6)} %select_n.14), kind=kOutput, calls=%fused_computation.1 | convolution fusion | flops 203423744 | bytes 6823940 | tf_op jit(solution)/shard_map/dot_general | solution.py:66
  270.1 74.5 %reduce-scatter.7.cloned.1.call-done = f32[32,48]{1,0:T(8,128)} async-done(((f32[512,48]{1,0:T(8,128)}), f32[32,48]{1,0:T(8,128)}) %reduce-scatter.7.cloned.1.call-update) | async-done | bytes 6160
  344.6 0.8 reshape.56
  345.5 0.7 copy.14
  346.2 94.1 %reduce-scatter.5.cloned.1.call-done = f32[3,512,16]{1,2,0:T(8,128)} async-done(((f32[3,8192,16]{1,2,0:T(8,128)}), f32[3,512,16]{1,2,0:T(8,128)}) %reduce-scatter.5.cloned.1.call-update) | async-done | bytes 98320 | tf_op jit(solution)/shard_map/reduce_scatter | solution.py:78
  (29 shorter events, 1.5 us)
Async XLA Ops:
  7.2 234.3 %copy-start = (bf16[128,8192]{1,0:T(8,128)(2,1)S(1)}, bf16[128,8192]{1,0:T(8,128)(2,1)}, u32[]{:S(2)}) copy-start(bf16[128,8192]{1,0:T(8,128)(2,1)} %param.8) | copy-start | bytes 6291460
  12.4 172.8 %copy-start.2 = (f32[3,16,32]{2,1,0:T(8,128)S(1)}, f32[3,16,32]{2,1,0:T(8,128)}, u32[]{:S(2)}) copy-start(f32[3,16,32]{2,1,0:T(8,128)} %param.11) | copy-start | bytes 18436
  12.4 174.3 %copy-start.1 = (bf16[128,512]{1,0:T(8,128)(2,1)S(1)}, bf16[128,512]{1,0:T(8,128)(2,1)}, u32[]{:S(2)}) copy-start(bf16[128,512]{1,0:T(8,128)(2,1)} %param.15) | copy-start | bytes 393220
  12.4 231.9 %all-to-all-start = ((bf16[32,256,512]{2,1,0:T(8,128)(2,1)}), bf16[32,256,512]{2,1,0:T(8,128)(2,1)}, u32[]{:S(2)}, u32[]{:S(2)}) async-start(bf16[32,256,512]{2,1,0:T(8,128)(2,1)} %stack.2), calls=%async_computation | async-start | bytes 16777216 | tf_op jit(solution)/shard_map/all_to_all | solution.py:38
  23.8 217.7 %copy-start.3 = (f32[128]{0:T(128)S(1)}, f32[128]{0:T(128)}, u32[]{:S(2)}) copy-start(f32[128]{0:T(128)} %param.12) | copy-start | bytes 1540
  23.8 217.7 %all-gather.2.cloned.1.call-start = ((), (), s32[]{:S(2)}) async-start(), calls=%async_computation.3 | async-start | bytes 1671168 | tf_op jit(solution)/shard_map/all_gather | solution.py:32
  24.5 320.1 %reduce-scatter.7.cloned.1.call-start = ((), (), s32[]{:S(2)}) async-start(), calls=%async_computation.5 | async-start | bytes 278528
  255.3 184.9 %reduce-scatter.5.cloned.1.call-start = ((), (), s32[]{:S(2)}) async-start(), calls=%async_computation.4 | async-start | bytes 1671168 | tf_op jit(solution)/shard_map/reduce_scatter | solution.py:78
Sparse Core Ops, SparseCore 0:
  27.6 73.3 all-gather.1
  255.5 89.1 reduce-scatter.6
  349.9 90.2 reduce-scatter.4
